TPU v7x, 32 devices: a whole 2x2x4 slice. The times are simulated.
32 devices in a mesh: dp: 4 (over y, core), table: 8 (over z, x).
Axes of the slice: x: 2, y: 2, z: 4, core: 2. Of those that a mesh axis runs over, the one named last changes fastest.
Arguments:
- table: float32 [131072, 256], P(('dp', 'table')), may hold values from -6 to 6
- hidden: float32 [16384, 256], P(('dp', 'table')), may hold values from -24 to 24
- neg_ids: int32 [4, 8, 4, 128], P('dp', 'table'), may hold values from 0 to 4095
- pos_ids: int32 [16384], P(('dp', 'table')), may hold values from 0 to 4095
- dloss: float32 [16384], P(('dp', 'table')), may hold values from -4 to 4
Outputs:
- row_loss: float32 [16384], P(('dp', 'table'))
- grad_hidden: float32 [16384, 256], P(('dp', 'table'))
- grad_table: float32 [131072, 256], P(('dp', 'table'))
All inputs are finite; a program needn't handle non-finite values.
Results may differ from a plain program's by a relative error of at most 0.0003.
Values sent between devices are 32-bit elements; how exact they have to be, the bound alone decides.
A program may use at most 192 MiB of HBM per device.

v0:
```python
import math
import jax
import jax.numpy as jnp
from jax import lax
from jax.sharding import PartitionSpec as P


def local(table, hidden, neg_ids, pos_ids, dloss):
    feat_width = hidden.shape[1]
    logit_scale = 3.0 / math.sqrt(feat_width)
    dp_peers = lax.axis_size("dp")
    table_index = lax.axis_index("table")
    local_ids = neg_ids[0, 0]
    per_peer = local_ids.shape[1]
    local_count = dp_peers * per_peer
    own_rows = hidden.shape[0]
    outgoing = table[local_ids.reshape(-1)].reshape(dp_peers, per_peer, feat_width)
    candidates = lax.all_to_all(outgoing, "dp", split_axis=0, concat_axis=0, tiled=True).reshape(
        local_count, feat_width
    )
    row_side = jnp.stack([pos_ids.astype(jnp.float32), dloss], axis=1)
    group_hidden, group_side = (
        lax.all_gather(hidden, "table", axis=0, tiled=True),
        lax.all_gather(row_side, "table", axis=0, tiled=True),
    )
    targets = group_side[:, 0].astype(jnp.int32)
    weights = group_side[:, 1]
    logits = logit_scale * lax.dot_general(
        group_hidden,
        candidates,
        (((1,), (1,)), ((), ())),
        precision=lax.Precision.HIGHEST,
        preferred_element_type=jnp.float32,
    )
    offsets = table_index * local_count + lax.iota(jnp.int32, local_count)
    target_hits = offsets[None, :] == targets[:, None]
    logit_part = jnp.sum(jnp.where(target_hits, logits, 0.0), axis=1)
    local_max = jnp.max(logits, axis=1)
    row_max = lax.pmax(local_max, "table")
    exponent = jnp.exp(logits - row_max[:, None])
    row_total, target_logit = lax.psum((jnp.sum(exponent, axis=1), logit_part), "table")
    group_loss = row_max + jnp.log(row_total) - target_logit
    row_loss = lax.dynamic_slice_in_dim(group_loss, table_index * own_rows, own_rows, 0)
    coefficient = (
        logit_scale
        * weights[:, None]
        * (exponent / row_total[:, None] - target_hits.astype(jnp.float32))
    )
    grad_hidden = lax.psum_scatter(
        jnp.dot(
            coefficient,
            candidates,
            precision=lax.Precision.HIGHEST,
            preferred_element_type=jnp.float32,
        ),
        "table",
        scatter_dimension=0,
        tiled=True,
    )
    cand_grad = lax.dot_general(
        coefficient,
        group_hidden,
        (((0,), (0,)), ((), ())),
        precision=lax.Precision.HIGHEST,
        preferred_element_type=jnp.float32,
    )
    returned = lax.all_to_all(
        cand_grad.reshape(dp_peers, per_peer, feat_width),
        "dp",
        split_axis=0,
        concat_axis=0,
        tiled=True,
    )
    grad_table = (
        jnp.zeros(table.shape, jnp.float32)
        .at[local_ids.reshape(-1)]
        .add(returned.reshape(local_count, feat_width))
    )
    return (row_loss, grad_hidden, grad_table)


def solution(mesh):
    in_specs = (
        P(("dp", "table"), None),
        P(("dp", "table"), None),
        P("dp", "table", None, None),
        P(("dp", "table")),
        P(("dp", "table")),
    )
    out_specs = (P(("dp", "table")), P(("dp", "table"), None), P(("dp", "table"), None))
    return jax.shard_map(local, mesh=mesh, in_specs=in_specs, out_specs=out_specs, check_vma=False)
```

profile of v0, /device:TPU:0, one launch (start us, length us, event | category | flops | bytes accessed | tf_op | source)
XLA Modules:
  0.0 280.4 jit_solution(1260502819999587651)
XLA Ops:
  7.2 0.0 all-gather.2.cloned.1.call-start
  7.2 0.7 all-gather.2.cloned.1.call-update
  7.9 0.7 compare_select_fusion.1
  8.6 4.4 %gather_fusion = f32[512,256]{1,0:T(8,128)} fusion(f32[4096,256]{1,0:T(8,128)} %param.5, s32[1024]{0:T(1024)S(1)} %pad_clamp_fusion), kind=kCustom, calls=%fused_computation | custom fusion | bytes 1050624 | tf_op jit(solution)/shard_map/gather | solution.py:17
  13.0 4.3 %all-to-all-start = ((f32[4,128,256]{2,1,0:T(8,128)}), f32[4,128,256]{2,1,0:T(8,128)S(1)}, u32[]{:S(2)}, u32[]{:S(2)}) async-start(f32[4,128,256]{2,1,0:T(8,128)} %bitcast.2), calls=%async_computation | async-start | bytes 1048576 | tf_op jit(solution)/shard_map/all_to_all | solution.py:18
  17.3 0.0 reduce-scatter.2.cloned.1.call-start
  17.3 0.7 convert_element_type.10
  18.0 0.7 pad_maximum_fusion
  18.7 32.5 %all_gather.7 = f32[4096,2]{0,1:T(2,128)S(1)} all-gather(f32[512,2]{0,1:T(2,128)S(1)} %pad_maximum_fusion), channel_id=1, replica_groups=mesh['dp'=4,'table'=8] {'table'}, dimensions={0}, use_global_device_ids=true | all-gather | bytes 36864 | tf_op jit(solution)/shard_map/all_gather | solution.py:24
  51.2 0.0 all-to-all-done
  51.2 34.7 %all-gather.2.cloned.1.call-done = f32[4096,256]{1,0:T(8,128)} async-done(((f32[512,256]{1,0:T(8,128)}), f32[4096,256]{1,0:T(8,128)}) %all-gather.2.cloned.1.call-update) | async-done | bytes 4194320 | tf_op jit(solution)/shard_map/all_gather | solution.py:23
  85.9 10.9 %multiply_reduce_fusion = (f32[4096]{0:T(1024)S(1)}, f32[512,4096]{1,0:T(8,128)}) fusion(f32[512,256]{1,0:T(8,128)S(1)} %bitcast.25, f32[4096,256]{1,0:T(8,128)} %all-gather.2.cloned.1.call-done), kind=kOutput, calls=%fused_computation.10 | convolution fusion | flops 6446641152 | bytes 13123584 | tf_op jit(solution)/shard_map/dot_general | solution.py:28
  96.8 34.7 %pmax.7 = f32[4096]{0:T(1024)S(1)} all-reduce(f32[4096]{0:T(1024)S(1)} %get-tuple-element.9), channel_id=1, replica_groups=mesh['dp'=4,'table'=8] {'table'}, use_global_device_ids=true, to_apply=%region_1.2 | all-reduce | flops 4096 | bytes 32768 | tf_op jit(solution)/shard_map/pmax | solution.py:39
  131.5 4.7 %fusion.4 = (f32[4096]{0:T(1024)S(1)}, f32[4096]{0:T(1024)S(1)}) fusion(f32[512,4096]{1,0:T(8,128)} %get-tuple-element.10, f32[4096]{0:T(1024)S(1)} %pmax.7, s32[4096]{0:T(1024)S(1)} %bitcast.28, s32[512]{0:T(512)S(1)} %iota_add_fusion), kind=kLoop, calls=%fused_computation.9 | loop fusion | flops 12574720 | bytes 8456192 | tf_op jit(solution)/shard_map/reduce_sum | solution.py:41
  136.2 33.2 %all-reduce = (f32[4096]{0:T(1024)S(1)}, f32[4096]{0:T(1024)S(1)}) all-reduce(f32[4096]{0:T(1024)S(1)} %get-tuple-element.4, f32[4096]{0:T(1024)S(1)} %get-tuple-element.3), channel_id=1, replica_groups=mesh['dp'=4,'table'=8] {'table'}, use_global_device_ids=true, to_apply=%region_5.6 | all-reduce | flops 8192 | bytes 65536 | tf_op jit(solution)/shard_map/psum | solution.py:41
  169.4 18.5 %fusion.9 = f32[4096,256]{1,0:T(8,128)} fusion(f32[512,256]{1,0:T(8,128)S(1)} %bitcast.26, f32[512,4096]{1,0:T(8,128)} %get-tuple-element.10, f32[4096]{0:T(1024)S(1)} %get-tuple-element.6, f32[4096]{0:T(1024)S(1)} %bitcast.31, s32[4096]{0:T(1024)S(1)} %bitcast.29, f32[4096]{0:T(1024)S(1)} %pmax.7, s32[512]{0:T(512)S(1)} %iota_add_fusion), kind=kOutput, calls=%fused_computation.23 | convolution fusion | flops 6457131008 | bytes 13174784 | tf_op jit(solution)/shard_map/dot_general | solution.py:50
  187.9 0.0 reduce-scatter.2.cloned.1.call-update
  187.9 14.0 %fusion.7 = f32[512,256]{1,0:T(8,128)} fusion(f32[4096,256]{1,0:T(8,128)} %all-gather.2.cloned.1.call-done, f32[512,4096]{1,0:T(8,128)} %get-tuple-element.10, f32[4096]{0:T(1024)S(1)} %get-tuple-element.6, f32[4096]{0:T(1024)S(1)} %bitcast.32, s32[4096]{0:T(1024)S(1)} %bitcast.30, f32[4096]{0:T(1024)S(1)} %pmax.7, s32[512]{0:T(512)S(1)} %iota_add_fusion), kind=kOutput, calls=%fused_computation.22 | convolution fusion | flops 6457131008 | bytes 13174784 | tf_op jit(solution)/shard_map/dot_general | solution.py:60
  202.0 3.5 %all-to-all-start.1 = ((f32[4,128,256]{2,1,0:T(8,128)}), f32[4,128,256]{2,1,0:T(8,128)S(1)}, u32[]{:S(2)}, u32[]{:S(2)}) async-start(f32[4,128,256]{2,1,0:T(8,128)} %bitcast.9), calls=%async_computation.2 | async-start | bytes 1048576 | tf_op jit(solution)/shard_map/all_to_all | solution.py:67
  205.4 0.7 dynamic-slice_subtract_fusion
  206.1 8.1 %all-to-all-done.1 = f32[4,128,256]{2,1,0:T(8,128)S(1)} async-done(((f32[4,128,256]{2,1,0:T(8,128)}), f32[4,128,256]{2,1,0:T(8,128)S(1)}, u32[]{:S(2)}, u32[]{:S(2)}) %all-to-all-start.1) | async-done | bytes 524320 | tf_op jit(solution)/shard_map/all_to_all | solution.py:67
  214.2 5.5 %scatter_custom_fusion = f32[4096,256]{1,0:T(8,128)} fusion(s32[512]{0:T(512)S(1)} %bitcast.34, f32[512,256]{1,0:T(8,128)S(1)} %bitcast.27, f32[]{:T(128)} %constant.11.clone.1), kind=kCustom, calls=%fused_computation.11 | custom fusion | flops 131072 | bytes 4194308 | tf_op jit(solution)/shard_map/scatter-add | solution.py:77
  219.8 53.8 %reduce-scatter.2.cloned.1.call-done = f32[512,256]{1,0:T(8,128)} async-done(((f32[4096,256]{1,0:T(8,128)}), f32[512,256]{1,0:T(8,128)}) %reduce-scatter.2.cloned.1.call-update) | async-done | bytes 524304 | tf_op jit(solution)/shard_map/reduce_scatter | solution.py:49
  (3 shorter events, 0.0 us)
Async XLA Ops:
  7.2 78.7 %all-gather.2.cloned.1.call-start = ((), (), s32[]{:S(2)}) async-start(), calls=%async_computation.3 | async-start | bytes 4718592 | tf_op jit(solution)/shard_map/all_gather | solution.py:23
  13.0 38.2 %all-to-all-start = ((f32[4,128,256]{2,1,0:T(8,128)}), f32[4,128,256]{2,1,0:T(8,128)S(1)}, u32[]{:S(2)}, u32[]{:S(2)}) async-start(f32[4,128,256]{2,1,0:T(8,128)} %bitcast.2), calls=%async_computation | async-start | bytes 1048576 | tf_op jit(solution)/shard_map/all_to_all | solution.py:18
  17.3 256.3 %reduce-scatter.2.cloned.1.call-start = ((), (), s32[]{:S(2)}) async-start(), calls=%async_computation.4 | async-start | bytes 4718592 | tf_op jit(solution)/shard_map/reduce_scatter | solution.py:49
  202.0 12.3 %all-to-all-start.1 = ((f32[4,128,256]{2,1,0:T(8,128)}), f32[4,128,256]{2,1,0:T(8,128)S(1)}, u32[]{:S(2)}, u32[]{:S(2)}) async-start(f32[4,128,256]{2,1,0:T(8,128)} %bitcast.9), calls=%async_computation.2 | async-start | bytes 1048576 | tf_op jit(solution)/shard_map/all_to_all | solution.py:67
Sparse Core Ops, SparseCore 0:
  10.1 75.7 all-gather.1
  188.0 85.4 reduce-scatter.1
where the time goes:
time: 281 us; the launch traced here: 280 us
  blocking collectives  100 us (36%)
  waiting for transfers between devices  97.3 us (35%)
  matrix products  43.4 us (15%)
  between operations  14.1 us (5%)
  other arithmetic  13 us (5%)
  starting transfers between devices  7.78 us (3%)
  local copies, waits for them, and re-layouts  4.42 us (2%)
    reduce_scatter x1, waiting for transfers between devices, local(): lax.psum_scatter(jnp.dot(coefficient, candidates, precision=lax.Precision...  53.8 us
    pmax x1, blocking collectives, local(): row_max = lax.pmax(local_max, 'table')  34.7 us
    all_gather x1, waiting for transfers between devices, local(): lax.all_gather(hidden, 'table', axis=0, tiled=True)  34.7 us
    psum x1, blocking collectives, local(): lax.psum((jnp.sum(exponent, axis=1), logit_part), 'table')  33.2 us
    all_gather x1, blocking collectives, local(): lax.all_gather(row_side, 'table', axis=0, tiled=True)  32.5 us
    dot_general x1, matrix products, local(): jnp.dot(coefficient, candidates, precision=lax.Precision.HIGHEST, preferr...  18.5 us
    dot_general x1, matrix products, local(): lax.dot_general(coefficient, group_hidden, (((0,), (0,)), ((), ())), prec...  14 us
    dot_general x1, matrix products, local(): lax.dot_general(group_hidden, candidates, (((1,), (1,)), ((), ())), preci...  10.9 us
  transfers between devices with their start and end apart: 4, of which 3 were waited for; matrix products, arithmetic and copies ran while one was open for 10% of the time, Pallas kernels for 0%

commit v1 on v0

--- a/solution.py
+++ b/solution.py
@@ -21,7 +21,9 @@
     row_side = jnp.stack([pos_ids.astype(jnp.float32), dloss], axis=1)
     group_hidden, group_side = (
         lax.all_gather(hidden, "table", axis=0, tiled=True),
-        lax.all_gather(row_side, "table", axis=0, tiled=True),
+        jnp.concatenate(
+            lax.all_to_all(jnp.stack([row_side] * lax.axis_size("table")), "table", 0, 0), axis=0
+        ),
     )
     targets = group_side[:, 0].astype(jnp.int32)
     weights = group_side[:, 1]

time: 281 us -> 281 us (level)
  blocking collectives: 100 us -> 67.9 us
  waiting for transfers between devices: 97.3 us -> 122 us
  starting transfers between devices: 7.78 us -> 14.3 us
    all_gather x1 -> x0, blocking collectives: 32.5 us -> none  [local(): lax.all_gather(row_side, 'table', axis=0, tiled=True)]
    all_gather x1, waiting for transfers between devices: 34.7 us -> 49.4 us  [local(): lax.all_gather(hidden, 'table', axis=0, tiled=True)]
    all_to_all x1, waiting for transfers between devices: 0.01 us -> 8.69 us  [local(): lax.all_to_all(outgoing, 'dp', split_axis=0, concat_axis=0, tiled=True)]
    all_to_all x0 -> x1, starting transfers between devices: none -> 7.28 us  [local(): lax.all_to_all(jnp.stack([row_side] * lax.axis_size('table')), 'table', 0...]
  transfers between devices with their start and end apart: 4 -> 5, of which waited for: 3 -> 5; matrix products, arithmetic and copies ran while one was open for 10% -> 10% of each run, Pallas kernels for 0% -> 0%
where the time goes in v1:
time: 281 us; the launch traced here: 280 us
  waiting for transfers between devices  122 us (43%)
  blocking collectives  67.9 us (24%)
  matrix products  43.4 us (15%)
  starting transfers between devices  14.3 us (5%)
  between operations  14.1 us (5%)
  other arithmetic  13 us (5%)
  local copies, waits for them, and re-layouts  5.11 us (2%)
    reduce_scatter x1, waiting for transfers between devices, local(): lax.psum_scatter(jnp.dot(coefficient, candidates, precision=lax.Precision...  53.8 us
    all_gather x1, waiting for transfers between devices, local(): lax.all_gather(hidden, 'table', axis=0, tiled=True)  49.4 us
    pmax x1, blocking collectives, local(): row_max = lax.pmax(local_max, 'table')  34.7 us
    psum x1, blocking collectives, local(): lax.psum((jnp.sum(exponent, axis=1), logit_part), 'table')  33.2 us
    dot_general x1, matrix products, local(): jnp.dot(coefficient, candidates, precision=lax.Precision.HIGHEST, preferr...  18.5 us
    dot_general x1, matrix products, local(): lax.dot_general(coefficient, group_hidden, (((0,), (0,)), ((), ())), prec...  14 us
    dot_general x1, matrix products, local(): lax.dot_general(group_hidden, candidates, (((1,), (1,)), ((), ())), preci...  10.9 us
    all_to_all x1, waiting for transfers between devices, local(): lax.all_to_all(outgoing, 'dp', split_axis=0, concat_axis=0, tiled=True)  8.69 us
  transfers between devices with their start and end apart: 5, of which 5 were waited for; matrix products, arithmetic and copies ran while one was open for 10% of the time, Pallas kernels for 0%

profile of v1, /device:TPU:0, one launch (start us, length us, event | category | flops | bytes accessed | tf_op | source)
XLA Modules:
  0.0 280.2 jit_solution(136171443852796749)
XLA Ops:
  7.2 0.0 all-gather.2.cloned.1.call-start
  7.2 0.7 all-gather.2.cloned.1.call-update
  7.9 0.7 convert_element_type.10
  8.6 0.7 pad_maximum_fusion
  9.3 0.6 stack.11
  9.9 7.3 %all-to-all-start.1 = ((f32[8,512,2]{1,2,0:T(2,128)}), f32[8,512,2]{1,2,0:T(2,128)S(1)}, u32[]{:S(2)}, u32[]{:S(2)}) async-start(f32[8,512,2]{1,2,0:T(2,128)} %stack.11), calls=%async_computation.1 | async-start | bytes 65536 | tf_op jit(solution)/shard_map/all_to_all | solution.py:25
  17.2 0.7 compare_select_fusion.1
  17.9 4.5 %gather_fusion = f32[512,256]{1,0:T(8,128)} fusion(f32[4096,256]{1,0:T(8,128)} %param.5, s32[1024]{0:T(1024)S(1)} %pad_clamp_fusion), kind=kCustom, calls=%fused_computation | custom fusion | bytes 1050624 | tf_op jit(solution)/shard_map/gather | solution.py:17
  22.4 1.6 all-to-all-done.1
  24.0 3.5 %all-to-all-start = ((f32[4,128,256]{2,1,0:T(8,128)}), f32[4,128,256]{2,1,0:T(8,128)S(1)}, u32[]{:S(2)}, u32[]{:S(2)}) async-start(f32[4,128,256]{2,1,0:T(8,128)} %bitcast.2), calls=%async_computation | async-start | bytes 1048576 | tf_op jit(solution)/shard_map/all_to_all | solution.py:18
  27.5 0.0 reduce-scatter.2.cloned.1.call-start
  27.5 8.7 %all-to-all-done = f32[4,128,256]{2,1,0:T(8,128)S(1)} async-done(((f32[4,128,256]{2,1,0:T(8,128)}), f32[4,128,256]{2,1,0:T(8,128)S(1)}, u32[]{:S(2)}, u32[]{:S(2)}) %all-to-all-start) | async-done | bytes 524320 | tf_op jit(solution)/shard_map/all_to_all | solution.py:18
  36.2 49.4 %all-gather.2.cloned.1.call-done = f32[4096,256]{1,0:T(8,128)} async-done(((f32[512,256]{1,0:T(8,128)}), f32[4096,256]{1,0:T(8,128)}) %all-gather.2.cloned.1.call-update) | async-done | bytes 4194320 | tf_op jit(solution)/shard_map/all_gather | solution.py:23
  85.6 10.9 %multiply_reduce_fusion = (f32[4096]{0:T(1024)S(1)}, f32[512,4096]{1,0:T(8,128)}) fusion(f32[512,256]{1,0:T(8,128)S(1)} %bitcast.26, f32[4096,256]{1,0:T(8,128)} %all-gather.2.cloned.1.call-done), kind=kOutput, calls=%fused_computation.10 | convolution fusion | flops 6446641152 | bytes 13123584 | tf_op jit(solution)/shard_map/dot_general | solution.py:30
  96.6 34.7 %pmax.7 = f32[4096]{0:T(1024)S(1)} all-reduce(f32[4096]{0:T(1024)S(1)} %get-tuple-element.9), channel_id=1, replica_groups=mesh['dp'=4,'table'=8] {'table'}, use_global_device_ids=true, to_apply=%region_1.2 | all-reduce | flops 4096 | bytes 32768 | tf_op jit(solution)/shard_map/pmax | solution.py:41
  131.3 4.7 %fusion.4 = (f32[4096]{0:T(1024)S(1)}, f32[4096]{0:T(1024)S(1)}) fusion(f32[512,4096]{1,0:T(8,128)} %get-tuple-element.10, f32[4096]{0:T(1024)S(1)} %pmax.7, s32[4096]{0:T(1024)S(1)} %bitcast.30, s32[512]{0:T(512)S(1)} %iota_add_fusion), kind=kLoop, calls=%fused_computation.9 | loop fusion | flops 12574720 | bytes 8456192 | tf_op jit(solution)/shard_map/reduce_sum | solution.py:43
  135.9 33.2 %all-reduce = (f32[4096]{0:T(1024)S(1)}, f32[4096]{0:T(1024)S(1)}) all-reduce(f32[4096]{0:T(1024)S(1)} %get-tuple-element.4, f32[4096]{0:T(1024)S(1)} %get-tuple-element.3), channel_id=1, replica_groups=mesh['dp'=4,'table'=8] {'table'}, use_global_device_ids=true, to_apply=%region_5.6 | all-reduce | flops 8192 | bytes 65536 | tf_op jit(solution)/shard_map/psum | solution.py:43
  169.2 18.5 %fusion.9 = f32[4096,256]{1,0:T(8,128)} fusion(f32[512,256]{1,0:T(8,128)S(1)} %bitcast.27, f32[512,4096]{1,0:T(8,128)} %get-tuple-element.10, f32[4096]{0:T(1024)S(1)} %get-tuple-element.6, f32[4096]{0:T(1024)S(1)} %bitcast.33, s32[4096]{0:T(1024)S(1)} %bitcast.31, f32[4096]{0:T(1024)S(1)} %pmax.7, s32[512]{0:T(512)S(1)} %iota_add_fusion), kind=kOutput, calls=%fused_computation.23 | convolution fusion | flops 6457131008 | bytes 13174784 | tf_op jit(solution)/shard_map/dot_general | solution.py:52
  187.6 0.0 reduce-scatter.2.cloned.1.call-update
  187.7 14.0 %fusion.7 = f32[512,256]{1,0:T(8,128)} fusion(f32[4096,256]{1,0:T(8,128)} %all-gather.2.cloned.1.call-done, f32[512,4096]{1,0:T(8,128)} %get-tuple-element.10, f32[4096]{0:T(1024)S(1)} %get-tuple-element.6, f32[4096]{0:T(1024)S(1)} %bitcast.34, s32[4096]{0:T(1024)S(1)} %bitcast.32, f32[4096]{0:T(1024)S(1)} %pmax.7, s32[512]{0:T(512)S(1)} %iota_add_fusion), kind=kOutput, calls=%fused_computation.22 | convolution fusion | flops 6457131008 | bytes 13174784 | tf_op jit(solution)/shard_map/dot_general | solution.py:62
  201.7 3.5 %all-to-all-start.2 = ((f32[4,128,256]{2,1,0:T(8,128)}), f32[4,128,256]{2,1,0:T(8,128)S(1)}, u32[]{:S(2)}, u32[]{:S(2)}) async-start(f32[4,128,256]{2,1,0:T(8,128)} %bitcast.10), calls=%async_computation.3 | async-start | bytes 1048576 | tf_op jit(solution)/shard_map/all_to_all | solution.py:69
  205.2 0.7 dynamic-slice_subtract_fusion
  205.9 8.1 %all-to-all-done.2 = f32[4,128,256]{2,1,0:T(8,128)S(1)} async-done(((f32[4,128,256]{2,1,0:T(8,128)}), f32[4,128,256]{2,1,0:T(8,128)S(1)}, u32[]{:S(2)}, u32[]{:S(2)}) %all-to-all-start.2) | async-done | bytes 524320 | tf_op jit(solution)/shard_map/all_to_all | solution.py:69
  214.0 5.5 %scatter_custom_fusion = f32[4096,256]{1,0:T(8,128)} fusion(s32[512]{0:T(512)S(1)} %bitcast.36, f32[512,256]{1,0:T(8,128)S(1)} %bitcast.28, f32[]{:T(128)} %constant.11.clone.1), kind=kCustom, calls=%fused_computation.11 | custom fusion | flops 131072 | bytes 4194308 | tf_op jit(solution)/shard_map/scatter-add | solution.py:79
  219.5 53.8 %reduce-scatter.2.cloned.1.call-done = f32[512,256]{1,0:T(8,128)} async-done(((f32[4096,256]{1,0:T(8,128)}), f32[512,256]{1,0:T(8,128)}) %reduce-scatter.2.cloned.1.call-update) | async-done | bytes 524304 | tf_op jit(solution)/shard_map/reduce_scatter | solution.py:51
  (3 shorter events, 0.0 us)
Async XLA Ops:
  7.2 78.5 %all-gather.2.cloned.1.call-start = ((), (), s32[]{:S(2)}) async-start(), calls=%async_computation.4 | async-start | bytes 4718592 | tf_op jit(solution)/shard_map/all_gather | solution.py:23
  9.9 14.1 %all-to-all-start.1 = ((f32[8,512,2]{1,2,0:T(2,128)}), f32[8,512,2]{1,2,0:T(2,128)S(1)}, u32[]{:S(2)}, u32[]{:S(2)}) async-start(f32[8,512,2]{1,2,0:T(2,128)} %stack.11), calls=%async_computation.1 | async-start | bytes 65536 | tf_op jit(solution)/shard_map/all_to_all | solution.py:25
  24.0 12.3 %all-to-all-start = ((f32[4,128,256]{2,1,0:T(8,128)}), f32[4,128,256]{2,1,0:T(8,128)S(1)}, u32[]{:S(2)}, u32[]{:S(2)}) async-start(f32[4,128,256]{2,1,0:T(8,128)} %bitcast.2), calls=%async_computation | async-start | bytes 1048576 | tf_op jit(solution)/shard_map/all_to_all | solution.py:18
  27.5 245.9 %reduce-scatter.2.cloned.1.call-start = ((), (), s32[]{:S(2)}) async-start(), calls=%async_computation.5 | async-start | bytes 4718592 | tf_op jit(solution)/shard_map/reduce_scatter | solution.py:51
  201.7 12.3 %all-to-all-start.2 = ((f32[4,128,256]{2,1,0:T(8,128)}), f32[4,128,256]{2,1,0:T(8,128)S(1)}, u32[]{:S(2)}, u32[]{:S(2)}) async-start(f32[4,128,256]{2,1,0:T(8,128)} %bitcast.10), calls=%async_computation.3 | async-start | bytes 1048576 | tf_op jit(solution)/shard_map/all_to_all | solution.py:69
Sparse Core Ops, SparseCore 0:
  10.1 75.4 all-gather.1
  187.8 85.5 reduce-scatter.1
